TPU v7x, 32 devices: a whole 2x2x4 slice. The times are simulated.
32 devices in a mesh: gx: 4 (over z), gy: 4 (over x, core), gz: 2 (over y).
Axes of the slice: x: 2, y: 2, z: 4, core: 2. Of those that a mesh axis runs over, the one named last changes fastest.
Arguments:
- activations: bfloat16 [1024, 8192], P('gy', 'gx'), may hold values from -0.5 to 0.5
- cotangent: bfloat16 [1024, 8192], P('gy', 'gx'), may hold values from -1.5 to 1.5
- gate_pre: bfloat16 [1024, 26624], P('gx', ('gy', 'gz')), may hold values from -6 to 6
- up_pre: bfloat16 [1024, 26624], P('gx', ('gy', 'gz')), may hold values from -6 to 6
- gate_weight: bfloat16 [8192, 26624], P('gx', ('gy', 'gz')), may hold values from -0.0625 to 0.0625
- up_weight: bfloat16 [8192, 26624], P('gx', ('gy', 'gz')), may hold values from -0.0625 to 0.0625
- down_weight: bfloat16 [26624, 8192], P(('gy', 'gz'), 'gx'), may hold values from -0.15625 to 0.15625
Outputs:
- input_grad: bfloat16 [1024, 8192], P('gy', 'gx')
- gate_grad: bfloat16 [8192, 26624], P('gx', ('gy', 'gz'))
- up_grad: bfloat16 [8192, 26624], P('gx', ('gy', 'gz'))
- down_grad: bfloat16 [26624, 8192], P(('gy', 'gz'), 'gx')
All inputs are finite; a program needn't handle non-finite values.
Results may differ from a plain program's by a relative error of at most 0.015.
Values may be sent and summed in bfloat16 or wider, within the bound.
A program may use at most 192 MiB of HBM per device.

v0:
```python
import jax
import jax.numpy as jnp
from jax import lax
from jax.sharding import PartitionSpec as P

over_rows = (((0,), (0,)), ((), ()))
over_cols = (((1,), (1,)), ((), ()))


def swiglu_grads(gate_in, up_in, grad_hidden):
    gate_val = gate_in.astype(jnp.float32)
    up_val = up_in.astype(jnp.float32)
    sigmoid = jax.nn.sigmoid(gate_val)
    hidden = (gate_val * sigmoid * up_val).astype(jnp.bfloat16)
    grad_gate = (grad_hidden * up_val * sigmoid * (1.0 + gate_val * (1.0 - sigmoid))).astype(
        jnp.bfloat16
    )
    grad_up = (grad_hidden * gate_val * sigmoid).astype(jnp.bfloat16)
    return (hidden, grad_gate, grad_up)


def input_terms(grad_gate, grad_up, gate_weight, up_weight):

    def compute(offset, amount):
        total = lax.dot_general(
            grad_gate, gate_weight, over_cols, preferred_element_type=jnp.float32
        )
        return total + lax.dot_general(
            grad_up, up_weight, over_cols, preferred_element_type=jnp.float32
        )

    return compute


def shards(activations, cotangent, gate_pre, up_pre, gate_weight, up_weight, down_weight):
    cotangent_all = lax.all_gather(cotangent, "gy", axis=0, tiled=True)
    gate_all, up_all = (
        lax.all_gather(gate_pre, "gx", axis=0, tiled=True),
        lax.all_gather(up_pre, "gx", axis=0, tiled=True),
    )
    local_sum = lax.dot_general(
        cotangent_all, down_weight, over_cols, preferred_element_type=jnp.float32
    )
    grad_hidden = lax.psum(local_sum, "gx")
    hidden, grad_gate, grad_up = swiglu_grads(gate_all, up_all, grad_hidden)
    down_grad = lax.dot_general(
        hidden, cotangent_all, over_rows, preferred_element_type=jnp.float32
    ).astype(jnp.bfloat16)
    segment = lax.all_gather(activations, "gy", axis=0, tiled=True)
    first = lax.dot_general(segment, grad_gate, over_rows, preferred_element_type=jnp.float32)
    second = lax.dot_general(segment, grad_up, over_rows, preferred_element_type=jnp.float32)
    row_count = activations.shape[0]
    terms = input_terms(grad_gate, grad_up, gate_weight, up_weight)
    share_rows = row_count // lax.axis_size("gz")
    input_share = lax.psum_scatter(
        terms(jnp.int32(0), lax.axis_size(("gy", "gz")) * share_rows),
        ("gy", "gz"),
        scatter_dimension=0,
        tiled=True,
    )
    input_grad = lax.all_gather(input_share.astype(jnp.bfloat16), "gz", axis=0, tiled=True)
    return (input_grad, first.astype(jnp.bfloat16), second.astype(jnp.bfloat16), down_grad)


def solution(mesh):
    in_specs = (
        P("gy", "gx"),
        P("gy", "gx"),
        P("gx", ("gy", "gz")),
        P("gx", ("gy", "gz")),
        P("gx", ("gy", "gz")),
        P("gx", ("gy", "gz")),
        P(("gy", "gz"), "gx"),
    )
    out_specs = (P("gy", "gx"), P("gx", ("gy", "gz")), P("gx", ("gy", "gz")), P(("gy", "gz"), "gx"))
    return jax.shard_map(shards, mesh=mesh, in_specs=in_specs, out_specs=out_specs, check_vma=False)
```

profile of v0, /device:TPU:0, one launch (start us, length us, event | category | flops | bytes accessed | tf_op | source)
XLA Modules:
  0.0 951.3 jit_solution(15693381875679629747)
XLA Ops:
  7.2 0.0 all-gather.6.cloned.1.call-start
  7.2 0.7 all-gather.6.cloned.1.call-update
  7.9 0.0 all-gather.10.cloned.1.call-start
  7.9 0.7 all-gather.10.cloned.1.call-update
  8.6 0.0 all-gather.8.cloned.1.call-start
  8.7 0.7 all-gather.8.cloned.1.call-update
  9.4 0.0 all-reduce.2.cloned.1.call-start
  9.4 37.3 %all-gather.6.cloned.1.call-done = bf16[1024,2048]{1,0:T(8,128)(2,1)} async-done(((bf16[256,2048]{1,0:T(8,128)(2,1)}), bf16[1024,2048]{1,0:T(8,128)(2,1)}) %all-gather.6.cloned.1.call-update) | async-done | bytes 4194320 | tf_op jit(solution)/shard_map/all_gather | solution.py:36
  46.8 22.5 %fusion.17 = f32[1024,3328]{1,0:T(8,128)} fusion(bf16[1024,2048]{1,0:T(8,128)(2,1)} %all-gather.6.cloned.1.call-done, bf16[3328,2048]{1,0:T(8,128)(2,1)} %param.13), kind=kOutput, calls=%fused_computation.24 | convolution fusion | flops 13958643712 | bytes 31457280 | tf_op jit(solution)/shard_map/dot_general | solution.py:41
  69.3 0.0 all-reduce.2.cloned.1.call-update
  69.3 0.0 all-gather.14.cloned.1.call-start
  69.4 0.5 all-gather.14.cloned.1.call-update
  69.9 0.2 reduce-scatter.2.cloned.1.call-start
  70.2 102.1 %all-gather.10.cloned.1.call-done = bf16[1024,3328]{1,0:T(8,128)(2,1)} async-done(((bf16[256,3328]{1,0:T(8,128)(2,1)}), bf16[1024,3328]{1,0:T(8,128)(2,1)}) %all-gather.10.cloned.1.call-update) | async-done | bytes 6815760 | tf_op jit(solution)/shard_map/all_gather | solution.py:38
  172.3 123.8 %all-gather.8.cloned.1.call-done = bf16[1024,3328]{1,0:T(8,128)(2,1)} async-done(((bf16[256,3328]{1,0:T(8,128)(2,1)}), bf16[1024,3328]{1,0:T(8,128)(2,1)}) %all-gather.8.cloned.1.call-update) | async-done | bytes 6815760 | tf_op jit(solution)/shard_map/all_gather | solution.py:39
  296.1 461.1 %all-reduce.2.cloned.1.call-done = f32[1024,3328]{1,0:T(8,128)} async-done(((f32[1024,3328]{1,0:T(8,128)}), f32[1024,3328]{1,0:T(8,128)}) %all-reduce.2.cloned.1.call-update) | async-done | bytes 13631504 | tf_op jit(solution)/shard_map/psum | solution.py:44
  757.1 12.2 %fusion.2 = bf16[1024,3328]{1,0:T(8,128)(2,1)S(1)} fusion(f32[1024,3328]{1,0:T(8,128)} %all-reduce.2.cloned.1.call-done, bf16[1024,3328]{1,0:T(8,128)(2,1)} %all-gather.8.cloned.1.call-done, bf16[1024,3328]{1,0:T(8,128)(2,1)} %all-gather.10.cloned.1.call-done), kind=kLoop, calls=%fused_computation.11 | loop fusion | flops 40894464 | bytes 34078720 | tf_op jit(solution)/shard_map/convert_element_type | solution.py:15
  769.3 0.0 copy-start
  769.3 2.9 copy-done
  772.2 18.1 %fusion.18 = f32[1024,2048]{1,0:T(8,128)} fusion(bf16[1024,3328]{1,0:T(8,128)(2,1)S(1)} %fusion.2, bf16[2048,3328]{1,0:T(8,128)(2,1)} %param.11), kind=kOutput, calls=%fused_computation.25 | convolution fusion | flops 13958643712 | bytes 28835840 | tf_op jit(solution)/shard_map/dot_general | solution.py:25
  790.3 24.1 %convolution_add_fusion = f32[1024,2048]{1,0:T(8,128)} fusion(f32[1024,2048]{1,0:T(8,128)} %fusion.18, bf16[2048,3328]{1,0:T(8,128)(2,1)} %param.12, f32[1024,3328]{1,0:T(8,128)} %all-reduce.2.cloned.1.call-done, bf16[1024,3328]{1,0:T(8,128)(2,1)} %all-gather.10.cloned.1.call-done), kind=kOutput, calls=%fused_computation.22 | convolution fusion | flops 13984595968 | bytes 50855936 | tf_op jit(solution)/shard_map/dot_general | solution.py:28
  814.4 0.0 reduce-scatter.2.cloned.1.call-update
  814.4 0.3 all-gather.12.cloned.1.call-start
  814.7 23.9 %convolution_convert_fusion = bf16[3328,2048]{1,0:T(8,128)(2,1)} fusion(bf16[1024,2048]{1,0:T(8,128)(2,1)} %all-gather.6.cloned.1.call-done, bf16[1024,3328]{1,0:T(8,128)(2,1)} %all-gather.8.cloned.1.call-done, bf16[1024,3328]{1,0:T(8,128)(2,1)} %all-gather.10.cloned.1.call-done), kind=kOutput, calls=%fused_computation.6 | convolution fusion | flops 13992722432 | bytes 31457280 | tf_op jit(solution)/shard_map/dot_general | solution.py:46
  838.6 0.0 all-gather.14.cloned.1.call-done
  838.6 23.5 %fusion.11 = bf16[2048,3328]{0,1:T(8,128)(2,1)} fusion(bf16[1024,2048]{1,0:T(8,128)(2,1)} %all-gather.14.cloned.1.call-done, f32[1024,3328]{1,0:T(8,128)} %all-reduce.2.cloned.1.call-done, bf16[1024,3328]{1,0:T(8,128)(2,1)} %all-gather.10.cloned.1.call-done), kind=kOutput, calls=%fused_computation.20 | convolution fusion | flops 13989314560 | bytes 38273024 | tf_op jit(solution)/shard_map/dot_general | solution.py:51
  862.1 22.0 %reduce-scatter.2.cloned.1.call-done = f32[128,2048]{1,0:T(8,128)} async-done(((f32[1024,2048]{1,0:T(8,128)}), f32[128,2048]{1,0:T(8,128)}) %reduce-scatter.2.cloned.1.call-update) | async-done | bytes 1048592 | tf_op jit(solution)/shard_map/reduce_scatter | solution.py:55
  884.1 2.1 convert_element_type.37
  886.2 0.0 all-gather.12.cloned.1.call-update
  886.2 21.0 %fusion.10 = bf16[2048,3328]{0,1:T(8,128)(2,1)} fusion(bf16[1024,3328]{1,0:T(8,128)(2,1)} %copy-done, bf16[1024,2048]{1,0:T(8,128)(2,1)} %all-gather.14.cloned.1.call-done), kind=kOutput, calls=%fused_computation.19 | convolution fusion | flops 13965459456 | bytes 24641536 | tf_op jit(solution)/shard_map/dot_general | solution.py:50
  907.3 17.4 %copy.11 = bf16[2048,3328]{1,0:T(8,128)(2,1)} copy(bf16[2048,3328]{0,1:T(8,128)(2,1)} %fusion.10) | data formatting | bytes 27262976
  924.7 17.4 %copy.12 = bf16[2048,3328]{1,0:T(8,128)(2,1)} copy(bf16[2048,3328]{0,1:T(8,128)(2,1)} %fusion.11) | data formatting | bytes 27262976
  942.1 0.0 all-gather.12.cloned.1.call-done
  942.2 2.3 copy.15
Async XLA Ops:
  7.2 39.6 %all-gather.6.cloned.1.call-start = ((), (), s32[]{:S(2)}) async-start(), calls=%async_computation.1 | async-start | bytes 5242880 | tf_op jit(solution)/shard_map/all_gather | solution.py:36
  7.9 164.4 %all-gather.10.cloned.1.call-start = ((), (), s32[]{:S(2)}) async-start(), calls=%async_computation.4 | async-start | bytes 8519680 | tf_op jit(solution)/shard_map/all_gather | solution.py:38
  8.6 287.4 %all-gather.8.cloned.1.call-start = ((), (), s32[]{:S(2)}) async-start(), calls=%async_computation.3 | async-start | bytes 8519680 | tf_op jit(solution)/shard_map/all_gather | solution.py:39
  9.4 747.8 %all-reduce.2.cloned.1.call-start = ((), (), s32[]{:S(2)}) async-start(), calls=%async_computation.2 | async-start | bytes 27262976 | tf_op jit(solution)/shard_map/psum | solution.py:44
  69.3 769.3 %all-gather.14.cloned.1.call-start = ((), (), s32[]{:S(2)}) async-start(), calls=%async_computation.7 | async-start | bytes 5242880 | tf_op jit(solution)/shard_map/all_gather | solution.py:49
  69.9 814.2 %reduce-scatter.2.cloned.1.call-start = ((), (), s32[]{:S(2)}) async-start(), calls=%async_computation.5 | async-start | bytes 9437184 | tf_op jit(solution)/shard_map/reduce_scatter | solution.py:55
  769.3 2.9 copy-start
  814.4 127.7 %all-gather.12.cloned.1.call-start = ((), (), s32[]{:S(2)}) async-start(), calls=%async_computation.6 | async-start | bytes 1572864 | tf_op jit(solution)/shard_map/all_gather | solution.py:61
Sparse Core Ops, SparseCore 0:
  9.6 37.1 all-gather.5
  48.3 123.9 all-gather.9
  173.9 122.1 all-gather.7
  299.0 458.1 all-reduce.1
  758.6 33.3 all-gather.13
  814.6 69.5 reduce-scatter.1
  886.4 21.2 all-gather.11
where the time goes:
time: 952 us; the launch traced here: 951 us
  waiting for transfers between devices  749 us (79%)
  matrix products  133 us (14%)
  local copies, waits for them, and re-layouts  40.1 us (4%)
  other arithmetic  14.3 us (2%)
  between operations  14.1 us (1%)
    psum x1, waiting for transfers between devices, shards(): grad_hidden = lax.psum(local_sum, 'gx')  461 us
    all_gather x1, waiting for transfers between devices, shards(): lax.all_gather(up_pre, 'gx', axis=0, tiled=True)  124 us
    all_gather x1, waiting for transfers between devices, shards(): lax.all_gather(gate_pre, 'gx', axis=0, tiled=True)  102 us
    unnamed x5, local copies, waits for them, and re-layouts  40.1 us
    all_gather x1, waiting for transfers between devices, shards(): cotangent_all = lax.all_gather(cotangent, 'gy', axis=0, tiled=True)  37.3 us
    dot_general x1, matrix products, compute(): lax.dot_general(grad_up, up_weight, over_cols, preferred_element_type=jnp...  24.1 us
    dot_general x1, matrix products, shards(): lax.dot_general(hidden, cotangent_all, over_rows, preferred_element_type=...  23.9 us
    dot_general x1, matrix products, shards(): lax.dot_general(segment, grad_up, over_rows, preferred_element_type=jnp.f...  23.5 us
  transfers between devices with their start and end apart: 7, of which 5 were waited for; matrix products, arithmetic and copies ran while one was open for 19% of the time, Pallas kernels for 0%

commit v1 on v0

--- a/solution.py
+++ b/solution.py
@@ -33,7 +33,20 @@
 
 
 def shards(activations, cotangent, gate_pre, up_pre, gate_weight, up_weight, down_weight):
-    cotangent_all = lax.all_gather(cotangent, "gy", axis=0, tiled=True)
+
+    def push_targets(frame, link_axis):
+        fan = jax.lax.axis_size(link_axis)
+        buffer = tuple(((dev, (dev + 1) % fan) for dev in range(fan)))
+
+        def solve_the_regions(outer):
+            if len(outer) == fan:
+                return outer
+            return solve_the_regions([jax.lax.ppermute(outer[0], link_axis, buffer), *outer])
+
+        y2 = jnp.concatenate(solve_the_regions([frame]), axis=0)
+        return jnp.roll(y2, (jax.lax.axis_index(link_axis) + 1) * frame.shape[0], axis=0)
+
+    cotangent_all = push_targets(cotangent, link_axis="gy")
     gate_all, up_all = (
         lax.all_gather(gate_pre, "gx", axis=0, tiled=True),
         lax.all_gather(up_pre, "gx", axis=0, tiled=True),

time: 952 us -> 922 us (0.968)
  waiting for transfers between devices: 749 us -> 701 us
  local copies, waits for them, and re-layouts: 40.1 us -> 50.8 us
    all_gather x1, waiting for transfers between devices: 102 us -> 49.4 us  [shards(): lax.all_gather(gate_pre, 'gx', axis=0, tiled=True)]
    ppermute x0 -> x3, waiting for transfers between devices: none -> 43.1 us  [solve_the_regions(): jax.lax.ppermute(outer[0], link_axis, buffer)]
    all_gather x1 -> x0, waiting for transfers between devices: 37.3 us -> none  [shards(): cotangent_all = lax.all_gather(cotangent, 'gy', axis=0, tiled=True)]
    unnamed x5 -> x14, local copies, waits for them, and re-layouts: 40.1 us -> 49.8 us
  transfers between devices with their start and end apart: 7 -> 9, of which waited for: 5 -> 7; matrix products, arithmetic and copies ran while one was open for 19% -> 21% of each run, Pallas kernels for 0% -> 0%
where the time goes in v1:
time: 922 us; the launch traced here: 915 us
  waiting for transfers between devices  701 us (76%)
  matrix products  133 us (14%)
  local copies, waits for them, and re-layouts  50.8 us (6%)
  between operations  14.4 us (2%)
  other arithmetic  14.2 us (2%)
    psum x1, waiting for transfers between devices, shards(): grad_hidden = lax.psum(local_sum, 'gx')  461 us
    all_gather x1, waiting for transfers between devices, shards(): lax.all_gather(up_pre, 'gx', axis=0, tiled=True)  124 us
    unnamed x14, local copies, waits for them, and re-layouts  49.8 us
    all_gather x1, waiting for transfers between devices, shards(): lax.all_gather(gate_pre, 'gx', axis=0, tiled=True)  49.4 us
    ppermute x3, waiting for transfers between devices, solve_the_regions(): jax.lax.ppermute(outer[0], link_axis, buffer)  43.1 us
    dot_general x1, matrix products, compute(): lax.dot_general(grad_up, up_weight, over_cols, preferred_element_type=jnp...  24.1 us
    dot_general x1, matrix products, shards(): lax.dot_general(hidden, cotangent_all, over_rows, preferred_element_type=...  24 us
    dot_general x1, matrix products, shards(): lax.dot_general(segment, grad_up, over_rows, preferred_element_type=jnp.f...  23.5 us
  transfers between devices with their start and end apart: 9, of which 7 were waited for; matrix products, arithmetic and copies ran while one was open for 21% of the time, Pallas kernels for 0%

profile of v1, /device:TPU:0, one launch (start us, length us, event | category | flops | bytes accessed | tf_op | source)
XLA Modules:
  0.0 915.5 jit_solution(8238232602193486680)
XLA Ops:
  7.2 0.0 copy-start.1
  7.2 0.0 all-gather.7.cloned.1.call-start
  7.2 0.7 all-gather.7.cloned.1.call-update
  7.9 0.0 all-gather.5.cloned.1.call-start
  8.0 0.7 all-gather.5.cloned.1.call-update
  8.7 0.0 all-reduce.2.cloned.1.call-start
  8.7 0.5 collective-permute-start
  9.2 14.6 %collective-permute-done = bf16[256,2048]{1,0:T(8,128)(2,1)S(1)} collective-permute-done((bf16[256,2048]{1,0:T(8,128)(2,1)}, bf16[256,2048]{1,0:T(8,128)(2,1)S(1)}, u32[]{:S(2)}, u32[]{:S(2)}) %collective-permute-start) | collective-permute-done | bytes 1048608 | tf_op jit(solution)/shard_map/ppermute | solution.py:44
  23.8 0.0 collective-permute-start.1
  23.9 14.2 %collective-permute-done.1 = bf16[256,2048]{1,0:T(8,128)(2,1)S(1)} collective-permute-done((bf16[256,2048]{1,0:T(8,128)(2,1)S(1)}, bf16[256,2048]{1,0:T(8,128)(2,1)S(1)}, u32[]{:S(2)}, u32[]{:S(2)}) %collective-permute-start.1) | collective-permute-done | bytes 1048608 | tf_op jit(solution)/shard_map/ppermute | solution.py:44
  38.1 0.0 collective-permute-start.2
  38.1 14.3 %collective-permute-done.2 = bf16[256,2048]{1,0:T(8,128)(2,1)} collective-permute-done((bf16[256,2048]{1,0:T(8,128)(2,1)S(1)}, bf16[256,2048]{1,0:T(8,128)(2,1)}, u32[]{:S(2)}, u32[]{:S(2)}) %collective-permute-start.2) | collective-permute-done | bytes 1048608 | tf_op jit(solution)/shard_map/ppermute | solution.py:44
  52.4 2.3 constant_dynamic-update-slice_fusion.7
  54.7 1.0 constant_dynamic-update-slice_fusion.6
  55.7 1.0 constant_dynamic-update-slice_fusion.5
  56.8 0.0 copy-done.1
  56.8 1.0 constant_dynamic-update-slice_fusion.4
  57.8 2.3 constant_dynamic-update-slice_fusion.3
  60.1 1.0 constant_dynamic-update-slice_fusion.2
  61.2 1.0 constant_dynamic-update-slice_fusion.1
  62.2 1.0 constant_dynamic-update-slice_fusion
  63.2 22.6 %fusion.15 = f32[1024,3328]{1,0:T(8,128)} fusion(bf16[3328,2048]{1,0:T(8,128)(2,1)} %param.13, bf16[2048,2048]{1,0:T(8,128)(2,1)} %constant_dynamic-update-slice_fusion, s32[]{:T(128)S(6)} %select_n.14), kind=kOutput, calls=%fused_computation.24 | convolution fusion | flops 13958643712 | bytes 31457284 | tf_op jit(solution)/shard_map/dot_general | solution.py:54
  85.9 0.0 all-reduce.2.cloned.1.call-update
  85.9 0.0 all-gather.11.cloned.1.call-start
  85.9 0.5 all-gather.11.cloned.1.call-update
  86.5 0.3 reduce-scatter.2.cloned.1.call-start
  86.8 49.4 %all-gather.7.cloned.1.call-done = bf16[1024,3328]{1,0:T(8,128)(2,1)} async-done(((bf16[256,3328]{1,0:T(8,128)(2,1)}), bf16[1024,3328]{1,0:T(8,128)(2,1)}) %all-gather.7.cloned.1.call-update) | async-done | bytes 6815760 | tf_op jit(solution)/shard_map/all_gather | solution.py:51
  136.2 123.8 %all-gather.5.cloned.1.call-done = bf16[1024,3328]{1,0:T(8,128)(2,1)} async-done(((bf16[256,3328]{1,0:T(8,128)(2,1)}), bf16[1024,3328]{1,0:T(8,128)(2,1)}) %all-gather.5.cloned.1.call-update) | async-done | bytes 6815760 | tf_op jit(solution)/shard_map/all_gather | solution.py:52
  260.0 461.2 %all-reduce.2.cloned.1.call-done = f32[1024,3328]{1,0:T(8,128)} async-done(((f32[1024,3328]{1,0:T(8,128)}), f32[1024,3328]{1,0:T(8,128)}) %all-reduce.2.cloned.1.call-update) | async-done | bytes 13631504 | tf_op jit(solution)/shard_map/psum | solution.py:57
  721.2 12.2 %fusion.2 = bf16[1024,3328]{1,0:T(8,128)(2,1)S(1)} fusion(f32[1024,3328]{1,0:T(8,128)} %all-reduce.2.cloned.1.call-done, bf16[1024,3328]{1,0:T(8,128)(2,1)} %all-gather.5.cloned.1.call-done, bf16[1024,3328]{1,0:T(8,128)(2,1)} %all-gather.7.cloned.1.call-done), kind=kLoop, calls=%fused_computation.11 | loop fusion | flops 40894464 | bytes 34078720 | tf_op jit(solution)/shard_map/convert_element_type | solution.py:15
  733.4 0.0 copy-start
  733.4 2.8 copy-done
  736.2 18.1 %fusion.22 = f32[1024,2048]{1,0:T(8,128)} fusion(bf16[1024,3328]{1,0:T(8,128)(2,1)S(1)} %fusion.2, bf16[2048,3328]{1,0:T(8,128)(2,1)} %param.11), kind=kOutput, calls=%fused_computation.37 | convolution fusion | flops 13958643712 | bytes 28835840 | tf_op jit(solution)/shard_map/dot_general | solution.py:25
  754.3 24.1 %convolution_add_fusion = f32[1024,2048]{1,0:T(8,128)} fusion(f32[1024,2048]{1,0:T(8,128)} %fusion.22, bf16[2048,3328]{1,0:T(8,128)(2,1)} %param.12, f32[1024,3328]{1,0:T(8,128)} %all-reduce.2.cloned.1.call-done, bf16[1024,3328]{1,0:T(8,128)(2,1)} %all-gather.7.cloned.1.call-done), kind=kOutput, calls=%fused_computation.22 | convolution fusion | flops 13984595968 | bytes 50855936 | tf_op jit(solution)/shard_map/dot_general | solution.py:28
  778.4 0.0 reduce-scatter.2.cloned.1.call-update
  778.5 0.6 all-gather.9.cloned.1.call-start
  779.0 24.0 %convolution_convert_fusion = bf16[3328,2048]{1,0:T(8,128)(2,1)} fusion(bf16[1024,3328]{1,0:T(8,128)(2,1)} %all-gather.5.cloned.1.call-done, bf16[1024,3328]{1,0:T(8,128)(2,1)} %all-gather.7.cloned.1.call-done, bf16[2048,2048]{1,0:T(8,128)(2,1)} %constant_dynamic-update-slice_fusion, s32[]{:T(128)S(6)} %select_n.14), kind=kOutput, calls=%fused_computation.6 | convolution fusion | flops 13992722432 | bytes 31457284 | tf_op jit(solution)/shard_map/dot_general | solution.py:59
  803.0 0.0 all-gather.11.cloned.1.call-done
  803.0 23.5 %fusion.11 = bf16[2048,3328]{0,1:T(8,128)(2,1)} fusion(bf16[1024,2048]{1,0:T(8,128)(2,1)} %all-gather.11.cloned.1.call-done, f32[1024,3328]{1,0:T(8,128)} %all-reduce.2.cloned.1.call-done, bf16[1024,3328]{1,0:T(8,128)(2,1)} %all-gather.7.cloned.1.call-done), kind=kOutput, calls=%fused_computation.20 | convolution fusion | flops 13989314560 | bytes 38273024 | tf_op jit(solution)/shard_map/dot_general | solution.py:64
  826.5 21.7 %reduce-scatter.2.cloned.1.call-done = f32[128,2048]{1,0:T(8,128)} async-done(((f32[1024,2048]{1,0:T(8,128)}), f32[128,2048]{1,0:T(8,128)}) %reduce-scatter.2.cloned.1.call-update) | async-done | bytes 1048592 | tf_op jit(solution)/shard_map/reduce_scatter | solution.py:68
  848.2 2.1 convert_element_type.37
  850.2 0.0 all-gather.9.cloned.1.call-update
  850.3 20.9 %fusion.10 = bf16[2048,3328]{0,1:T(8,128)(2,1)} fusion(bf16[1024,3328]{1,0:T(8,128)(2,1)} %copy-done, bf16[1024,2048]{1,0:T(8,128)(2,1)} %all-gather.11.cloned.1.call-done), kind=kOutput, calls=%fused_computation.19 | convolution fusion | flops 13965459456 | bytes 24641536 | tf_op jit(solution)/shard_map/dot_general | solution.py:63
  871.2 17.4 %copy.12 = bf16[2048,3328]{1,0:T(8,128)(2,1)} copy(bf16[2048,3328]{0,1:T(8,128)(2,1)} %fusion.11) | data formatting | bytes 27262976
  888.6 17.4 %copy.11 = bf16[2048,3328]{1,0:T(8,128)(2,1)} copy(bf16[2048,3328]{0,1:T(8,128)(2,1)} %fusion.10) | data formatting | bytes 27262976
  906.1 0.0 all-gather.9.cloned.1.call-done
  906.1 2.3 copy.22
Async XLA Ops:
  7.2 49.6 %copy-start.1 = (bf16[256,2048]{1,0:T(8,128)(2,1)S(1)}, bf16[256,2048]{1,0:T(8,128)(2,1)}, u32[]{:S(2)}) copy-start(bf16[256,2048]{1,0:T(8,128)(2,1)} %param.8) | copy-start | bytes 3145732
  7.2 129.1 %all-gather.7.cloned.1.call-start = ((), (), s32[]{:S(2)}) async-start(), calls=%async_computation.3 | async-start | bytes 8519680 | tf_op jit(solution)/shard_map/all_gather | solution.py:51
  7.9 252.1 %all-gather.5.cloned.1.call-start = ((), (), s32[]{:S(2)}) async-start(), calls=%async_computation.2 | async-start | bytes 8519680 | tf_op jit(solution)/shard_map/all_gather | solution.py:52
  8.7 712.6 %all-reduce.2.cloned.1.call-start = ((), (), s32[]{:S(2)}) async-start(), calls=%async_computation.1 | async-start | bytes 27262976 | tf_op jit(solution)/shard_map/psum | solution.py:57
  8.7 15.1 %collective-permute-start = (bf16[256,2048]{1,0:T(8,128)(2,1)}, bf16[256,2048]{1,0:T(8,128)(2,1)S(1)}, u32[]{:S(2)}, u32[]{:S(2)}) collective-permute-start(bf16[256,2048]{1,0:T(8,128)(2,1)} %param.8), channel_id=1, source_target_pairs={{0,2},{2,4},{4,6},{6,0},{1,3},{3,5},{5,7},{7,1},{8,10},{10,12},{12... | collective-permute-start | bytes 3145736 | tf_op jit(solution)/shard_map/ppermute | solution.py:44
  23.8 14.2 %collective-permute-start.1 = (bf16[256,2048]{1,0:T(8,128)(2,1)S(1)}, bf16[256,2048]{1,0:T(8,128)(2,1)S(1)}, u32[]{:S(2)}, u32[]{:S(2)}) collective-permute-start(bf16[256,2048]{1,0:T(8,128)(2,1)S(1)} %collective-permute-done), channel_id=1, source_target_pairs={{0,2},{2,4},{4,6},{6,0},{1,3},{3,5},{5,7},{7,1},{8,10},{10,12},{12... | collective-permute-start | bytes 3145736 | tf_op jit(solution)/shard_map/ppermute | solution.py:44
  38.1 14.3 %collective-permute-start.2 = (bf16[256,2048]{1,0:T(8,128)(2,1)S(1)}, bf16[256,2048]{1,0:T(8,128)(2,1)}, u32[]{:S(2)}, u32[]{:S(2)}) collective-permute-start(bf16[256,2048]{1,0:T(8,128)(2,1)S(1)} %collective-permute-done.1), channel_id=1, source_target_pairs={{0,2},{2,4},{4,6},{6,0},{1,3},{3,5},{5,7},{7,1},{8,10},{10,12},{12... | collective-permute-start | bytes 3145736 | tf_op jit(solution)/shard_map/ppermute | solution.py:44
  85.9 717.1 %all-gather.11.cloned.1.call-start = ((), (), s32[]{:S(2)}) async-start(), calls=%async_computation.6 | async-start | bytes 5242880 | tf_op jit(solution)/shard_map/all_gather | solution.py:62
  86.5 761.7 %reduce-scatter.2.cloned.1.call-start = ((), (), s32[]{:S(2)}) async-start(), calls=%async_computation.4 | async-start | bytes 9437184 | tf_op jit(solution)/shard_map/reduce_scatter | solution.py:68
  733.4 2.8 copy-start
  778.5 127.6 %all-gather.9.cloned.1.call-start = ((), (), s32[]{:S(2)}) async-start(), calls=%async_computation.5 | async-start | bytes 1572864 | tf_op jit(solution)/shard_map/all_gather | solution.py:74
Sparse Core Ops, SparseCore 0:
  9.6 126.6 all-gather.6
  137.8 122.1 all-gather.4
  263.1 458.1 all-reduce.1
  722.6 33.3 all-gather.10
  778.6 69.5 reduce-scatter.1
  850.4 21.2 all-gather.8
